TPU v7x, 32 devices: a whole 2x2x4 slice. The times are simulated.
32 devices in a mesh: space: 4 (over y, x), slot: 8 (over z, core).
Axes of the slice: x: 2, y: 2, z: 4, core: 2. Of those that a mesh axis runs over, the one named last changes fastest.
Arguments:
- control: bfloat16 [1536, 1024], P('slot', 'space'), may hold values from -6 to 6
- block_lists: int32 [32, 2], P('space'), may hold values from 0 to 7, all different within a row; in each aligned block of 8 rows (0 to 7, 8 to 15, ...) at most 2 rows name the same one
- loc_tiles: bfloat16 [32, 2, 128, 128], P('space'), may hold values from -0.375 to 0.375
- ensemble: bfloat16 [8, 1536, 4096], P('slot', None, 'space'), may hold values from -2.5 to 2.5
- obs_col: int32 [8, 8192], P('slot', 'space'), may hold values from 0 to 4095, as said below
- obs_wts: float32 [8, 48, 8192], P('slot', None, 'space'), may hold values from -0.875 to 0.875
- innovation: float32 [8, 8192], P('slot', 'space'), may hold values from -6 to 6
- inv_error: float32 [8, 8192], P('slot', 'space'), may hold values from 1 to 16
Outputs:
- first_grad: float32 [1536, 1024], P('slot', 'space')
- second_grad: float32 [1536, 1024], P('slot', 'space')
Inputs may be any that keep to these rules, and one draw needn't show every extreme that they name: `block_lists`: each grid block lists 2 different control blocks; among the grid blocks of one space index no control block is listed more than twice. `obs_col`: observation j lies in grid columns (j // 2048) * 8 * 128 to that plus 8 * 128 - 1.
All inputs are finite; a program needn't handle non-finite values.
Results may differ from a plain program's by a relative error of at most 0.0003.
Values may be sent and summed in bfloat16 or wider, within the bound.
A program may use at most 64 MiB of HBM per device.

v0:
```python
import jax
import jax.numpy as jnp
from jax import lax
from jax.sharding import PartitionSpec as P

LEV = 48
BLOCK = 128
K = 2


descent_step = 0.5


def per_device(control, block_lists, loc_tiles, ensemble, obs_col, obs_wts, innovation, inv_error):
    member_rows = control.shape[0]
    cell_count = ensemble.shape[2]
    space_count = lax.axis_size("space")
    block_total = control.shape[1] // BLOCK * space_count
    ref_ids = block_lists.reshape(-1)
    tiles_wide = loc_tiles.astype(jnp.float32)
    tiles_flat = tiles_wide.reshape(-1, BLOCK, BLOCK)
    selector = (ref_ids[:, None] == jnp.arange(block_total, dtype=jnp.int32)[None, :]).astype(
        jnp.float32
    )
    local_cols = obs_col[0] - lax.axis_index("space") * cell_count
    pick_table = (jnp.arange(cell_count, dtype=jnp.int32)[:, None] == local_cols[None, :]).astype(
        jnp.float32
    )
    weights = obs_wts[0]
    inverse = inv_error[0]
    observed = innovation[0]
    own_slot = ensemble[0]

    def localize(current):
        gathered = lax.all_gather(current.astype(jnp.float32), "space", axis=1, tiled=True)
        picked = gathered.reshape(member_rows, block_total, BLOCK)[:, ref_ids, :]
        products = jnp.einsum("crj,rij->cri", picked, tiles_flat, precision=lax.Precision.HIGHEST)
        return (
            products.reshape(member_rows, -1, K, BLOCK).sum(axis=2).reshape(member_rows, cell_count)
        )

    def observe(increment):
        seen_values = jnp.dot(increment, pick_table, precision=lax.Precision.HIGHEST)
        modelled = jnp.sum(weights * seen_values, axis=0)
        residual = inverse * (modelled - observed)
        return jnp.dot(weights * residual[None, :], pick_table.T, precision=lax.Precision.HIGHEST)

    def gradient(current):
        updates = localize(current)
        all_updates = lax.all_gather(updates, "slot", axis=0, tiled=True)
        product_full = own_slot.astype(jnp.float32) * all_updates
        increment = jnp.sum(product_full.reshape(-1, LEV, cell_count), axis=0)
        adjoint_obs = observe(increment)
        forcing = lax.psum_scatter(
            own_slot.astype(jnp.float32)
            * jnp.tile(adjoint_obs, (member_rows * lax.axis_size("slot") // LEV, 1)),
            "slot",
            scatter_dimension=0,
            tiled=True,
        )
        grid_cells = forcing.reshape(member_rows, -1, BLOCK)
        products = jnp.einsum(
            "cgi,gkij->cgkj", grid_cells, tiles_wide, precision=lax.Precision.HIGHEST
        )
        control_term = jnp.einsum(
            "rb,crj->cbj",
            selector,
            products.reshape(member_rows, -1, BLOCK),
            precision=lax.Precision.HIGHEST,
        )
        returned = lax.psum_scatter(
            control_term.reshape(member_rows, block_total * BLOCK),
            "space",
            scatter_dimension=1,
            tiled=True,
        )
        return current.astype(jnp.float32) + returned

    first_grad = gradient(control)
    stepped = control.astype(jnp.float32) - descent_step * first_grad
    second_grad = gradient(stepped)
    return (first_grad, second_grad)


def solution(mesh):
    placed = (
        P("slot", "space"),
        P("space", None),
        P("space", None, None, None),
        P("slot", None, "space"),
        P("slot", "space"),
        P("slot", None, "space"),
        P("slot", "space"),
        P("slot", "space"),
    )
    return jax.shard_map(
        per_device,
        mesh=mesh,
        in_specs=placed,
        out_specs=(P("slot", "space"), P("slot", "space")),
        check_vma=False,
    )
```

profile of v0, /device:TPU:0, one launch (start us, length us, event | category | flops | bytes accessed | tf_op | source)
XLA Modules:
  0.0 419.0 jit_solution(14871258517747074934)
XLA Ops:
  7.2 0.8 copy.38
  8.1 0.9 convert_element_type.7
  9.0 12.7 %all_gather.12 = f32[192,1024]{1,0:T(8,128)S(1)} all-gather(f32[192,256]{1,0:T(8,128)S(1)} %convert_element_type.7), channel_id=1, replica_groups=mesh['space'=4,'slot'=8] {'space'}, dimensions={1}, use_global_device_ids=true | all-gather | bytes 983040 | tf_op jit(solution)/shard_map/all_gather | solution.py:35
  22.4 1.1 bitcast_reduce_fusion.1
  23.6 1.0 copy_bitcast_fusion.3
  24.6 65.1 %all-gather.3.cloned.1.call-done = f32[1536,1024]{1,0:T(8,128)} async-done(((f32[192,1024]{1,0:T(8,128)}), f32[1536,1024]{1,0:T(8,128)}) %all-gather.3.cloned.1.call-update) | async-done | bytes 6291472 | tf_op jit(solution)/shard_map/all_gather | solution.py:50
  89.8 8.0 %convert_multiply_fusion.3 = f32[1536,1024]{1,0:T(8,128)} fusion(f32[1536,1024]{1,0:T(8,128)} %all-gather.3.cloned.1.call-done, bf16[1,1536,1024]{2,1,0:T(8,128)(2,1)} %param.11), kind=kLoop, calls=%fused_computation.5 | loop fusion | flops 3145728 | bytes 15728640 | tf_op jit(solution)/shard_map/mul | solution.py:51
  97.8 3.2 reduce_sum.59
  101.1 3.2 fusion.19
  104.3 4.2 %fusion.2 = f32[48,1024]{1,0:T(8,128)S(1)} fusion(s32[2048]{0:T(1024)S(1)} %bitcast.114, f32[1,48,2048]{2,1,0:T(8,128)S(1)} %copy-done.7, f32[2048]{0:T(1024)S(1)} %bitcast.119), kind=kOutput, calls=%fused_computation.9 | convolution fusion | flops 1210155008 | bytes 606208 | tf_op jit(solution)/shard_map/dot_general | solution.py:46
  108.5 3.6 convert_multiply_fusion.2
  112.4 68.3 %reduce-scatter.5.cloned.1.call-done = f32[192,1024]{1,0:T(8,128)} async-done(((f32[1536,1024]{1,0:T(8,128)}), f32[192,1024]{1,0:T(8,128)}) %reduce-scatter.5.cloned.1.call-update) | async-done | bytes 786448 | tf_op jit(solution)/shard_map/reduce_scatter | solution.py:54
  180.7 1.3 copy.58
  182.8 1.5 fusion.16
  184.3 1.0 copy.77
  185.4 24.6 %reduce-scatter.7.cloned.1.call-done = f32[192,256]{1,0:T(8,128)} async-done(((f32[192,1024]{1,0:T(8,128)}), f32[192,256]{1,0:T(8,128)}) %reduce-scatter.7.cloned.1.call-update) | async-done | bytes 196624 | tf_op jit(solution)/shard_map/reduce_scatter | solution.py:71
  210.0 1.6 multiply_subtract_fusion
  211.6 11.1 %all_gather.14 = f32[192,1024]{1,0:T(8,128)S(1)} all-gather(f32[192,256]{1,0:T(8,128)S(1)} %get-tuple-element.2), channel_id=1, replica_groups=mesh['space'=4,'slot'=8] {'space'}, dimensions={1}, use_global_device_ids=true | all-gather | bytes 983040 | tf_op jit(solution)/shard_map/all_gather | solution.py:35
  223.4 1.1 bitcast_reduce_fusion
  224.6 1.0 copy_bitcast_fusion.2
  225.6 64.9 %all-gather.5.cloned.1.call-done = f32[1536,1024]{1,0:T(8,128)} async-done(((f32[192,1024]{1,0:T(8,128)}), f32[1536,1024]{1,0:T(8,128)}) %all-gather.5.cloned.1.call-update) | async-done | bytes 6291472 | tf_op jit(solution)/shard_map/all_gather | solution.py:50
  290.5 8.0 %convert_multiply_fusion.1 = f32[1536,1024]{1,0:T(8,128)} fusion(f32[1536,1024]{1,0:T(8,128)} %all-gather.5.cloned.1.call-done, bf16[1,1536,1024]{2,1,0:T(8,128)(2,1)} %param.11), kind=kLoop, calls=%fused_computation.3 | loop fusion | flops 3145728 | bytes 15728640 | tf_op jit(solution)/shard_map/mul | solution.py:51
  298.5 3.2 reduce_sum.63
  301.7 3.2 fusion.18
  304.9 4.2 %fusion = f32[48,1024]{1,0:T(8,128)S(1)} fusion(s32[2048]{0:T(1024)S(1)} %bitcast.116, f32[1,48,2048]{2,1,0:T(8,128)S(1)} %copy-done.7, f32[2048]{0:T(1024)S(1)} %bitcast.117), kind=kOutput, calls=%fused_computation.7 | convolution fusion | flops 1210155008 | bytes 606208 | tf_op jit(solution)/shard_map/dot_general | solution.py:46
  309.1 3.6 convert_multiply_fusion
  312.8 68.6 %reduce-scatter.9.cloned.1.call-done = f32[192,1024]{1,0:T(8,128)} async-done(((f32[1536,1024]{1,0:T(8,128)}), f32[192,1024]{1,0:T(8,128)}) %reduce-scatter.9.cloned.1.call-update) | async-done | bytes 786448 | tf_op jit(solution)/shard_map/reduce_scatter | solution.py:54
  381.3 1.3 copy.60
  383.4 1.5 fusion.14
  384.9 1.0 copy.76
  385.9 24.6 %reduce-scatter.11.cloned.1.call-done = f32[192,256]{1,0:T(8,128)} async-done(((f32[192,1024]{1,0:T(8,128)}), f32[192,256]{1,0:T(8,128)}) %reduce-scatter.11.cloned.1.call-update) | async-done | bytes 196624 | tf_op jit(solution)/shard_map/reduce_scatter | solution.py:71
  410.6 1.6 add.27
  (41 shorter events, 3.8 us)
Async XLA Ops:
  7.2 15.2 %copy-start = (bf16[8,2,128,128]{3,2,1,0:T(8,128)(2,1)S(1)}, bf16[8,2,128,128]{3,2,1,0:T(8,128)(2,1)}, u32[]{:S(2)}) copy-start(bf16[8,2,128,128]{3,2,1,0:T(8,128)(2,1)} %param.10) | copy-start | bytes 1572868
  7.2 82.6 %all-gather.3.cloned.1.call-start = ((), (), s32[]{:S(2)}) async-start(), calls=%async_computation.4 | async-start | bytes 7077888 | tf_op jit(solution)/shard_map/all_gather | solution.py:50
  22.4 2.2 copy-start.6
  24.6 156.2 %reduce-scatter.5.cloned.1.call-start = ((), (), s32[]{:S(2)}) async-start(), calls=%async_computation.5 | async-start | bytes 7077888 | tf_op jit(solution)/shard_map/reduce_scatter | solution.py:54
  97.8 3.3 copy-start.7
  101.0 3.2 copy-start.4
  101.0 3.2 copy-start.5
  101.1 7.5 %copy-start.1 = (bf16[1,1536,1024]{2,1,0:T(8,128)(2,1)S(1)}, bf16[1,1536,1024]{2,1,0:T(8,128)(2,1)}, u32[]{:S(2)}) copy-start(bf16[1,1536,1024]{2,1,0:T(8,128)(2,1)} %param.11) | copy-start | bytes 9437188
  112.1 97.9 %reduce-scatter.7.cloned.1.call-start = ((), (), s32[]{:S(2)}) async-start(), calls=%async_computation.6 | async-start | bytes 983040 | tf_op jit(solution)/shard_map/reduce_scatter | solution.py:71
  182.8 27.2 %copy-start.3 = (bf16[192,256]{1,0:T(8,128)(2,1)S(1)}, bf16[192,256]{1,0:T(8,128)(2,1)}, u32[]{:S(2)}) copy-start(bf16[192,256]{1,0:T(8,128)(2,1)} %param.8) | copy-start | bytes 294916
  185.4 105.1 %all-gather.5.cloned.1.call-start = ((), (), s32[]{:S(2)}) async-start(), calls=%async_computation.7 | async-start | bytes 7077888 | tf_op jit(solution)/shard_map/all_gather | solution.py:50
  225.6 155.7 %reduce-scatter.9.cloned.1.call-start = ((), (), s32[]{:S(2)}) async-start(), calls=%async_computation.8 | async-start | bytes 7077888 | tf_op jit(solution)/shard_map/reduce_scatter | solution.py:54
  301.7 7.4 %copy-start.2 = (bf16[1,1536,1024]{2,1,0:T(8,128)(2,1)S(1)}, bf16[1,1536,1024]{2,1,0:T(8,128)(2,1)}, u32[]{:S(2)}) copy-start(bf16[1,1536,1024]{2,1,0:T(8,128)(2,1)} %param.11) | copy-start | bytes 9437188
  312.7 97.9 %reduce-scatter.11.cloned.1.call-start = ((), (), s32[]{:S(2)}) async-start(), calls=%async_computation.9 | async-start | bytes 983040 | tf_op jit(solution)/shard_map/reduce_scatter | solution.py:71
Sparse Core Ops, SparseCore 0:
  24.7 65.0 all-gather.2
  112.2 68.4 reduce-scatter.4
  185.5 24.4 reduce-scatter.6
  225.7 64.7 all-gather.4
  312.8 68.4 reduce-scatter.8
  386.1 24.4 reduce-scatter.10
where the time goes:
time: 419 us
  waiting for transfers between devices  316 us (75%)
  other arithmetic  33.8 us (8%)
  blocking collectives  23.7 us (6%)
  matrix products  21.6 us (5%)
  between operations  14.4 us (3%)
  local copies, waits for them, and re-layouts  8.98 us (2%)
    reduce_scatter x2, waiting for transfers between devices, gradient(): lax.psum_scatter(own_slot.astype(jnp.float32) * jnp.tile(adjoint_obs, (me...  137 us
    all_gather x2, waiting for transfers between devices, gradient(): all_updates = lax.all_gather(updates, 'slot', axis=0, tiled=True)  130 us
    reduce_scatter x2, waiting for transfers between devices, gradient(): lax.psum_scatter(control_term.reshape(member_rows, block_total * BLOCK),...  49.2 us
    all_gather x2, blocking collectives, localize(): lax.all_gather(current.astype(jnp.float32), 'space', axis=1, tiled=True)  23.7 us
    mul x2, other arithmetic, gradient(): product_full = own_slot.astype(jnp.float32) * all_updates  16 us
    dot_general x2, matrix products, observe(): jnp.dot(weights * residual[None, :], pick_table.T, precision=lax.Precisio...  8.41 us
  transfers between devices with their start and end apart: 6, of which 6 were waited for; matrix products, arithmetic and copies ran while one was open for 0% of the time, Pallas kernels for 0%

commit v1 on v0

v1 whole, which is shorter than its diff:
```python
import jax
import jax.numpy as jnp
from jax import lax
from jax.sharding import PartitionSpec as P

LEV = 48
BLOCK = 128
K = 2
descent_step = 0.5
F32 = jnp.float32
BF16 = jnp.bfloat16


def parts(x):
    high = lax.reduce_precision(x, 8, 7)
    low = lax.reduce_precision(x - high, 8, 7)
    return high.astype(BF16), low.astype(BF16)


def mm(a, b, dims):
    return lax.dot_general(a, b, (dims, ((), ())), preferred_element_type=F32)


def mm2(x, b, dims):
    high, low = parts(x)
    return mm(high, b, dims) + mm(low, b, dims)


def per_device(control, block_lists, loc_tiles, ensemble, obs_col, obs_wts, innovation, inv_error):
    rows = control.shape[0]
    cells = ensemble.shape[2]
    slots = lax.axis_size("slot")
    blocks = control.shape[1] // BLOCK * lax.axis_size("space")
    local_cols = obs_col[0] - lax.axis_index("space") * cells
    pick = (jnp.arange(cells, dtype=jnp.int32)[:, None] == local_cols[None, :]).astype(BF16)
    weights, inverse, observed = obs_wts[0], inv_error[0], innovation[0]
    spread = lax.all_to_all(ensemble.reshape(slots, rows, cells), "slot", 0, 0)
    spread = spread.reshape(slots, rows // LEV, LEV, cells)
    chosen = block_lists[:, :, None] == jnp.arange(blocks, dtype=jnp.int32)
    dense = jnp.sum(
        jnp.where(chosen[..., None, None], loc_tiles[:, :, None], 0), axis=1, dtype=BF16
    )
    dense = dense.transpose(0, 2, 1, 3).reshape(cells, blocks * BLOCK)

    def gradient(updates, base):
        updates = updates.reshape(1, rows // LEV, LEV, cells)
        partial = jnp.sum(spread.astype(F32) * updates, axis=1)
        increment = lax.psum_scatter(partial, "slot", scatter_dimension=0, tiled=True)[0]
        seen = mm2(increment, pick, ((1,), (0,)))
        residual = inverse * (jnp.sum(weights * seen, axis=0) - observed)
        adjoint = mm2(weights * residual[None], pick, ((1,), (1,)))
        everyone = lax.all_gather(adjoint, "slot", axis=0)
        forcing = jnp.sum(spread.astype(F32) * everyone[:, None], axis=0).reshape(rows, cells)
        term = mm2(forcing, dense, ((1,), (0,)))
        return base + lax.psum_scatter(term, "space", scatter_dimension=1, tiled=True)

    whole = lax.all_gather(control, "space", axis=1, tiled=True)
    wide = control.astype(F32)
    first = gradient(mm(whole, dense, ((1,), (1,))), wide)
    stepped = wide - descent_step * first
    whole = lax.all_gather(stepped, "space", axis=1, tiled=True)
    second = gradient(mm2(whole, dense, ((1,), (1,))), stepped)
    return first, second


def solution(mesh):
    placed = (
        P("slot", "space"),
        P("space", None),
        P("space", None, None, None),
        P("slot", None, "space"),
        P("slot", "space"),
        P("slot", None, "space"),
        P("slot", "space"),
        P("slot", "space"),
    )
    return jax.shard_map(
        per_device,
        mesh=mesh,
        in_specs=placed,
        out_specs=(P("slot", "space"), P("slot", "space")),
        check_vma=False,
    )
```

time: 419 us -> 314 us (0.75)
  waiting for transfers between devices: 316 us -> 218 us
  other arithmetic: 33.8 us -> 22.1 us
  local copies, waits for them, and re-layouts: 8.98 us -> 1.5 us
  starting transfers between devices: 0.43 us -> 6.76 us
  matrix products: 21.6 us -> 26.5 us
    all_gather x2, waiting for transfers between devices: 130 us -> 46 us  [gradient(): everyone = lax.all_gather(adjoint, 'slot', axis=0)]
    reduce_scatter x4, waiting for transfers between devices: 186 us -> 119 us  [the longest x2 67.5 us: gradient(): lax.psum_scatter(partial, 'slot', scatter_dimension=0, tiled=True)[0]]
    all_to_all x0 -> x1, waiting for transfers between devices: none -> 52.9 us  [per_device(): spread = lax.all_to_all(ensemble.reshape(slots, rows, cells), 'slot', 0, 0)]
    mul x6 -> x2, other arithmetic: 23.2 us -> 0.03 us  [gradient(): residual = inverse * (jnp.sum(weights * seen, axis=0) - observed)]
    reduce_sum x2 -> x5, other arithmetic: 6.41 us -> 18.7 us  [the longest x2 11.2 us: gradient(): partial = jnp.sum(spread.astype(F32) * updates, axis=1)]
    all_to_all x0 -> x1, starting transfers between devices: none -> 6.34 us  [per_device(): spread = lax.all_to_all(ensemble.reshape(slots, rows, cells), 'slot', 0, 0)]
    unnamed x21 -> x27, local copies, waits for them, and re-layouts: 5.45 us -> 0.14 us
    dot_general x10 -> x15, matrix products: 21.6 us -> 26.5 us  [mm(): return lax.dot_general(a, b, (dims, ((), ())), preferred_element_type=F32)]
  transfers between devices with their start and end apart: 6 -> 7, of which waited for: 6 -> 7; matrix products, arithmetic and copies ran while one was open for 0% -> 2% of each run, Pallas kernels for 0% -> 0%
where the time goes in v1:
time: 314 us; the launch traced here: 313 us
  waiting for transfers between devices  218 us (69%)
  matrix products  26.5 us (8%)
  blocking collectives  23.8 us (8%)
  other arithmetic  22.1 us (7%)
  between operations  14.4 us (5%)
  starting transfers between devices  6.76 us (2%)
    reduce_scatter x2, waiting for transfers between devices, gradient(): lax.psum_scatter(partial, 'slot', scatter_dimension=0, tiled=True)[0]  67.5 us
    all_to_all x1, waiting for transfers between devices, per_device(): spread = lax.all_to_all(ensemble.reshape(slots, rows, cells), 'slot', 0, 0)  52.9 us
    reduce_scatter x2, waiting for transfers between devices, gradient(): lax.psum_scatter(term, 'space', scatter_dimension=1, tiled=True)  51.5 us
    all_gather x2, waiting for transfers between devices, gradient(): everyone = lax.all_gather(adjoint, 'slot', axis=0)  46 us
    dot_general x15, matrix products, mm(): return lax.dot_general(a, b, (dims, ((), ())), preferred_element_type=F32)  26.5 us
    all_gather x1, blocking collectives, per_device(): whole = lax.all_gather(control, 'space', axis=1, tiled=True)  12.7 us
    reduce_sum x2, other arithmetic, gradient(): partial = jnp.sum(spread.astype(F32) * updates, axis=1)  11.2 us
    all_gather x1, blocking collectives, per_device(): whole = lax.all_gather(stepped, 'space', axis=1, tiled=True)  11.1 us
  transfers between devices with their start and end apart: 7, of which 7 were waited for; matrix products, arithmetic and copies ran while one was open for 2% of the time, Pallas kernels for 0%

profile of v1, /device:TPU:0, one launch (start us, length us, event | category | flops | bytes accessed | tf_op | source)
XLA Modules:
  0.0 313.3 jit_solution(16380479060691610687)
XLA Ops:
  7.2 6.3 %all-to-all-start = ((bf16[8,192,1024]{2,1,0:T(8,128)(2,1)}), bf16[8,192,1024]{2,1,0:T(8,128)(2,1)S(1)}, u32[]{:S(2)}, u32[]{:S(2)}) async-start(bf16[8,192,1024]{2,1,0:T(8,128)(2,1)} %bitcast.83), calls=%async_computation | async-start | bytes 6291456 | tf_op jit(solution)/shard_map/all_to_all | solution.py:37
  13.7 2.5 select_reduce_fusion
  16.2 1.4 copy.13
  17.6 12.7 %all_gather.18 = bf16[192,1024]{1,0:T(8,128)(2,1)S(1)} all-gather(bf16[192,256]{1,0:T(8,128)(2,1)S(1)} %copy-done.4), channel_id=1, replica_groups=mesh['space'=4,'slot'=8] {'space'}, dimensions={1}, use_global_device_ids=true | all-gather | bytes 491520 | tf_op jit(solution)/shard_map/all_gather | solution.py:57
  30.4 1.7 fusion.34
  32.1 52.9 %all-to-all-done = bf16[8,192,1024]{2,1,0:T(8,128)(2,1)S(1)} async-done(((bf16[8,192,1024]{2,1,0:T(8,128)(2,1)}), bf16[8,192,1024]{2,1,0:T(8,128)(2,1)S(1)}, u32[]{:S(2)}, u32[]{:S(2)}) %all-to-all-start) | async-done | bytes 3145760 | tf_op jit(solution)/shard_map/all_to_all | solution.py:37
  85.1 6.1 %multiply_reduce_fusion.1 = (f32[8,48,1024]{2,1,0:T(8,128)}, f32[8,4,48,1024]{3,2,1,0:T(8,128)}) fusion(f32[4,48,1024]{2,1,0:T(8,128)} %bitcast.87, bf16[8,4,48,1024]{3,2,1,0:T(8,128)(2,1)S(1)} %bitcast.74), kind=kLoop, calls=%fused_computation.14 | loop fusion | flops 4325376 | bytes 11796480 | tf_op jit(solution)/shard_map/reduce_sum | solution.py:47
  91.2 33.2 %reduce-scatter.5.cloned.1.call-done = f32[1,48,1024]{2,1,0:T(8,128)} async-done(((f32[8,48,1024]{2,1,0:T(8,128)}), f32[1,48,1024]{2,1,0:T(8,128)}) %reduce-scatter.5.cloned.1.call-update) | async-done | bytes 196624 | tf_op jit(solution)/shard_map/reduce_scatter | solution.py:48
  124.4 2.7 fusion.6
  127.1 1.8 fusion.45
  128.9 1.7 fusion.4
  130.7 2.4 fusion.47
  133.3 22.9 %all-gather.5.cloned.1.call-done = f32[384,1024]{1,0:T(8,128)} async-done(((f32[48,1024]{1,0:T(8,128)}), f32[384,1024]{1,0:T(8,128)}) %all-gather.5.cloned.1.call-update) | async-done | bytes 1572880 | tf_op jit(solution)/shard_map/all_gather | solution.py:52
  156.3 2.5 fusion.9
  158.8 0.6 fusion.30
  159.4 1.5 fusion.36
  161.0 25.7 %reduce-scatter.7.cloned.1.call-done = f32[192,256]{1,0:T(8,128)} async-done(((f32[192,1024]{1,0:T(8,128)}), f32[192,256]{1,0:T(8,128)}) %reduce-scatter.7.cloned.1.call-update) | async-done | bytes 196624 | tf_op jit(solution)/shard_map/reduce_scatter | solution.py:55
  186.7 1.6 convert_subtract_fusion
  188.4 11.1 %all_gather.21 = f32[192,1024]{1,0:T(8,128)S(1)} all-gather(f32[192,256]{1,0:T(8,128)S(1)} %get-tuple-element.2), channel_id=1, replica_groups=mesh['space'=4,'slot'=8] {'space'}, dimensions={1}, use_global_device_ids=true | all-gather | bytes 983040 | tf_op jit(solution)/shard_map/all_gather | solution.py:61
  199.5 2.6 fusion.26
  202.1 0.9 fusion.39
  202.9 5.1 %multiply_reduce_fusion = f32[8,48,1024]{2,1,0:T(8,128)} fusion(f32[8,4,48,1024]{3,2,1,0:T(8,128)} %get-tuple-element.5, f32[4,48,1024]{2,1,0:T(8,128)S(1)} %bitcast.84), kind=kLoop, calls=%fused_computation.13 | loop fusion | flops 2752512 | bytes 8650752 | tf_op jit(solution)/shard_map/reduce_sum | solution.py:47
  208.1 34.4 %reduce-scatter.9.cloned.1.call-done = f32[1,48,1024]{2,1,0:T(8,128)} async-done(((f32[8,48,1024]{2,1,0:T(8,128)}), f32[1,48,1024]{2,1,0:T(8,128)}) %reduce-scatter.9.cloned.1.call-update) | async-done | bytes 196624 | tf_op jit(solution)/shard_map/reduce_scatter | solution.py:48
  242.5 2.7 fusion.2
  245.2 1.8 fusion.46
  247.0 1.7 fusion
  248.7 2.4 fusion.48
  251.2 23.1 %all-gather.7.cloned.1.call-done = f32[384,1024]{1,0:T(8,128)} async-done(((f32[48,1024]{1,0:T(8,128)}), f32[384,1024]{1,0:T(8,128)}) %all-gather.7.cloned.1.call-update) | async-done | bytes 1572880 | tf_op jit(solution)/shard_map/all_gather | solution.py:52
  274.3 2.5 fusion.8
  277.5 1.5 fusion.42
  279.0 25.8 %reduce-scatter.11.cloned.1.call-done = f32[192,256]{1,0:T(8,128)} async-done(((f32[192,1024]{1,0:T(8,128)}), f32[192,256]{1,0:T(8,128)}) %reduce-scatter.11.cloned.1.call-update) | async-done | bytes 196624 | tf_op jit(solution)/shard_map/reduce_scatter | solution.py:55
  304.8 1.6 add.43
  (44 shorter events, 1.4 us)
Async XLA Ops:
  7.2 6.4 %copy-start.8 = (s32[8,2]{0,1:T(2,128)S(1)}, s32[8,2]{0,1:T(2,128)}, u32[]{:S(2)}) copy-start(s32[8,2]{0,1:T(2,128)} %param.9) | copy-start | bytes 196
  7.2 77.9 %all-to-all-start = ((bf16[8,192,1024]{2,1,0:T(8,128)(2,1)}), bf16[8,192,1024]{2,1,0:T(8,128)(2,1)S(1)}, u32[]{:S(2)}, u32[]{:S(2)}) async-start(bf16[8,192,1024]{2,1,0:T(8,128)(2,1)} %bitcast.83), calls=%async_computation | async-start | bytes 6291456 | tf_op jit(solution)/shard_map/all_to_all | solution.py:37
  13.5 110.9 %reduce-scatter.5.cloned.1.call-start = ((), (), s32[]{:S(2)}) async-start(), calls=%async_computation.5 | async-start | bytes 1769472 | tf_op jit(solution)/shard_map/reduce_scatter | solution.py:48
  16.2 1.4 copy-start.4
  17.6 12.7 %copy-start = (bf16[8,128,8,128]{3,2,1,0:T(8,128)(2,1)}, bf16[8,128,8,128]{3,2,1,0:T(8,128)(2,1)S(1)}, u32[]{:S(2)}) copy-start(bf16[8,128,8,128]{3,2,1,0:T(8,128)(2,1)S(1)} %copy.13) | copy-start | bytes 6291460
  85.0 6.1 %copy-start.7 = (s32[1,2048]{1,0:T(1,128)S(1)}, s32[1,2048]{1,0:T(1,128)}, u32[]{:S(2)}) copy-start(s32[1,2048]{1,0:T(1,128)} %param.12) | copy-start | bytes 24580
  91.1 65.1 %all-gather.5.cloned.1.call-start = ((), (), s32[]{:S(2)}) async-start(), calls=%async_computation.9 | async-start | bytes 1769472 | tf_op jit(solution)/shard_map/all_gather | solution.py:52
  124.4 2.7 copy-start.9
  124.4 2.7 copy-start.11
  127.1 1.8 copy-start.5
  127.1 1.8 copy-start.6
  133.1 53.6 %reduce-scatter.7.cloned.1.call-start = ((), (), s32[]{:S(2)}) async-start(), calls=%async_computation.6 | async-start | bytes 983040 | tf_op jit(solution)/shard_map/reduce_scatter | solution.py:55
  156.3 2.6 copy-start.1
  161.0 81.5 %reduce-scatter.9.cloned.1.call-start = ((), (), s32[]{:S(2)}) async-start(), calls=%async_computation.7 | async-start | bytes 1769472 | tf_op jit(solution)/shard_map/reduce_scatter | solution.py:48
  199.5 2.6 copy-start.2
  208.1 66.3 %all-gather.7.cloned.1.call-start = ((), (), s32[]{:S(2)}) async-start(), calls=%async_computation.10 | async-start | bytes 1769472 | tf_op jit(solution)/shard_map/all_gather | solution.py:52
  242.5 2.7 copy-start.10
  242.5 2.7 copy-start.12
  251.2 53.6 %reduce-scatter.11.cloned.1.call-start = ((), (), s32[]{:S(2)}) async-start(), calls=%async_computation.8 | async-start | bytes 983040 | tf_op jit(solution)/shard_map/reduce_scatter | solution.py:55
  274.3 2.6 copy-start.3
Sparse Core Ops, SparseCore 0:
  91.3 33.0 reduce-scatter.4
  133.2 22.9 all-gather.4
  161.1 25.6 reduce-scatter.6
  208.2 34.2 reduce-scatter.8
  251.3 22.9 all-gather.6
  279.1 25.6 reduce-scatter.10

commit v2 on v1

v2 whole, which is shorter than its diff:
```python
import functools

import jax
import jax.numpy as jnp
from jax import lax
from jax.experimental import pallas as pl
from jax.experimental.pallas import tpu as pltpu
from jax.sharding import PartitionSpec as P

LEV = 48
BLOCK = 128
CORES = 2
CHUNK = 256
OBS_CHUNK = 512
descent_step = 0.5
F32 = jnp.float32
BF16 = jnp.bfloat16
MESH = pl.DeviceIdType.MESH


def halves(x):
    high = x.astype(BF16)
    return high, (x - high.astype(F32)).astype(BF16)


def dot(a, b):
    return lax.dot_general(a, b, (((1,), (0,)), ((), ())), preferred_element_type=F32)


def dot_t(a, b):
    return lax.dot_general(a, b, (((1,), (1,)), ((), ())), preferred_element_type=F32)


def kernel(
    spaces, slots,
    control, lists, tiles, ensemble, cols, wts, innovation, inverse,
    first_ref, second_ref,
    ens, dense, pick, updates, adjsum, forced, out_a, in_a, sums, in_b, adj, term, term_in, step_src,
    ctl_in, step_in,
    local_sem, ens_s, ens_r, a_s, a_r, b_s, b_r, c_s, c_r, d_s, d_r, g_s, g_r, t_s, t_r,
):
    rows, width = control.shape
    cells = ensemble.shape[2]
    nobs = cols.shape[1]
    chips = slots // CORES
    members = rows // LEV
    me = lax.axis_index("space")
    slot = lax.axis_index("slot")
    z, core = slot // CORES, lax.rem(slot, CORES)
    sibling = slot + 1 - 2 * core

    def slot_at(dz, dk):
        zz = lax.rem(z + dz + chips, chips)
        return zz * CORES + (core if dk == 0 else 1 - core)

    def space_at(d):
        return lax.rem(me + d + spaces, spaces)

    barrier = pltpu.get_barrier_semaphore()
    for dz in range(chips):
        for dk in range(CORES):
            if dz or dk:
                pl.semaphore_signal(
                    barrier, inc=1, device_id={"slot": slot_at(dz, dk)}, device_id_type=MESH
                )
    for d in range(1, spaces):
        pl.semaphore_signal(barrier, inc=1, device_id={"space": space_at(d)}, device_id_type=MESH)
    pl.semaphore_wait(barrier, slots - 1 + spaces - 1)

    def send(src, dst, ssem, rsem, where):
        copy = pltpu.make_async_remote_copy(
            src_ref=src, dst_ref=dst, send_sem=ssem, recv_sem=rsem,
            device_id=where, device_id_type=MESH,
        )
        copy.start()
        return copy

    gathers = [
        send(control, ctl_in.at[d - 1], g_s.at[0, d - 1], g_r.at[0, d - 1], {"space": space_at(d)})
        for d in range(1, spaces)
    ]
    moved = {}
    for dz in sorted(range(chips), key=lambda v: -min(v, chips - v)):
        for dk in range(CORES):
            if dz or dk:
                rel = dz * CORES + dk
                to = slot_at(dz, dk)
                moved[rel] = send(
                    ensemble.at[0, pl.ds(pl.multiple_of(to * rows, rows), rows)],
                    ens.at[rel], ens_s.at[rel - 1], ens_r.at[rel - 1], {"slot": to},
                )
    own = pltpu.make_async_copy(
        ensemble.at[0, pl.ds(pl.multiple_of(slot * rows, rows), rows)], ens.at[0], local_sem
    )
    own.start()

    per = width // BLOCK

    def build_dense(g, carry):
        one = lists[g, 0]
        two = lists[g, 1]
        tile_one = tiles[g, 0].astype(F32)
        tile_two = tiles[g, 1].astype(F32)
        at = pl.ds(pl.multiple_of(g * BLOCK, BLOCK), BLOCK)
        for b in range(spaces * per):
            mask_one = jnp.where(one == b, 1.0, 0.0)
            mask_two = jnp.where(two == b, 1.0, 0.0)
            value = tile_one * mask_one + tile_two * mask_two
            dense[b // per, at, (b % per) * BLOCK : (b % per + 1) * BLOCK] = value.astype(BF16)
        return carry

    lax.fori_loop(0, cells // BLOCK, build_dense, 0)

    first_cell = me * cells

    def build_pick(q, carry):
        line = cols[:, pl.ds(pl.multiple_of(q * OBS_CHUNK, OBS_CHUNK), OBS_CHUNK)] - first_cell

        def band(r, inner):
            rowid = lax.broadcasted_iota(jnp.int32, (BLOCK, OBS_CHUNK), 0) + r * BLOCK
            hot = jnp.where(rowid == line, 1.0, 0.0).astype(BF16)
            pick[q, pl.ds(pl.multiple_of(r * BLOCK, BLOCK), BLOCK)] = hot
            return inner

        return lax.fori_loop(0, cells // BLOCK, band, carry)

    lax.fori_loop(0, nobs // OBS_CHUNK, build_pick, 0)

    def chunks(body):
        def run(c, carry):
            body(pl.ds(pl.multiple_of(c * CHUNK, CHUNK), CHUNK))
            return carry

        lax.fori_loop(0, cells // CHUNK, run, 0)

    def project(rel, at):
        total = None
        for m in range(members):
            lev = slice(m * LEV, (m + 1) * LEV)
            value = ens[rel, lev, at].astype(F32) * updates[lev, at]
            total = value if total is None else total + value
        return total

    def gradient(i, base):
        sent = []
        copies_a = {}
        for dz in list(range(1, chips)) + [0]:
            rel = dz * CORES + 1
            if i == 0:
                moved[rel].wait_recv()

            def fill(at, rel=rel, dz=dz):
                out_a[i, dz, :, at] = project(rel, at)

            chunks(fill)
            copies_a[dz] = send(
                out_a.at[i, dz], in_a.at[i, dz], a_s.at[i, dz], a_r.at[i, dz], {"slot": sibling}
            )
        copies_b = {}
        for dz in list(range(1, chips)) + [0]:
            rel = dz * CORES
            if i == 0:
                if rel:
                    moved[rel].wait_recv()
                else:
                    own.wait()
            copies_a[dz].wait_recv()

            def fold(at, rel=rel, dz=dz):
                sums[i, dz, :, at] = project(rel, at) + in_a[i, dz, :, at]

            chunks(fold)
            if dz:
                copies_b[dz] = send(
                    sums.at[i, dz], in_b.at[i, dz - 1], b_s.at[i, dz - 1], b_r.at[i, dz - 1],
                    {"slot": slot_at(-dz, 0)},
                )
        for dz in range(1, chips):
            copies_b[dz].wait_recv()
        increment = sums[i, 0]
        for dz in range(1, chips):
            increment = increment + in_b[i, dz - 1]
        high, low = halves(increment)
        pair = jnp.concatenate([high, low], axis=0)
        adjsum[...] = jnp.zeros_like(adjsum)

        def observe(q, carry):
            at = pl.ds(pl.multiple_of(q * OBS_CHUNK, OBS_CHUNK), OBS_CHUNK)
            table = pick[q]
            seen = dot(pair, table)
            seen = seen[:LEV] + seen[LEV:]
            w = wts[0, :, at]
            modelled = jnp.sum(w * seen, axis=0, keepdims=True)
            residual = inverse[:, at] * (modelled - innovation[:, at])
            up, down = halves(w * residual)
            back = dot_t(jnp.concatenate([up, down], axis=0), table)
            adjsum[...] += back[:LEV] + back[LEV:]
            return carry

        lax.fori_loop(0, nobs // OBS_CHUNK, observe, 0)
        adj[i, 0] = adjsum[...]
        copies_c = {}
        for dz in list(range(1, chips)):
            copies_c[dz] = send(
                adj.at[i, 0], adj.at[i, dz * CORES], c_s.at[i, dz], c_r.at[i, dz],
                {"slot": slot_at(dz, 0)},
            )
        copies_c[0] = send(
            adj.at[i, 0], adj.at[i, 1], c_s.at[i, 0], c_r.at[i, 0], {"slot": sibling}
        )
        copies_d = {}
        for dz in range(1, chips):
            copies_c[dz].wait_recv()
            copies_d[dz] = send(
                adj.at[i, dz * CORES], adj.at[i, dz * CORES + 1], d_s.at[i, dz - 1],
                d_r.at[i, dz - 1], {"slot": sibling},
            )
        copies_c[0].wait_recv()
        for dz in range(1, chips):
            copies_d[dz].wait_recv()

        def force(at):
            for m in range(members):
                lev = slice(m * LEV, (m + 1) * LEV)
                total = ens[0, lev, at].astype(F32) * adj[i, 0, :, at]
                for rel in range(1, slots):
                    total = total + ens[rel, lev, at].astype(F32) * adj[i, rel, :, at]
                up, down = halves(total)
                forced[lev, at] = up
                forced[rows + m * LEV : rows + (m + 1) * LEV, at] = down

        chunks(force)
        copies_t = []
        for d in range(1, spaces):
            to = space_at(d)
            both = dot(forced[...], dense[to])
            term[i, d - 1] = both[:rows] + both[rows:]
            copies_t.append(
                send(
                    term.at[i, d - 1], term_in.at[i, d - 1], t_s.at[i, d - 1], t_r.at[i, d - 1],
                    {"space": to},
                )
            )
        both = dot(forced[...], dense[me])
        total = base + both[:rows] + both[rows:]
        for d in range(1, spaces):
            copies_t[d - 1].wait_recv()
            total = total + term_in[i, d - 1]
        sent += list(copies_a.values()) + list(copies_b.values()) + list(copies_c.values())
        sent += list(copies_d.values()) + copies_t
        return total, sent

    value = dot_t(control[...], dense[me])
    for d in range(1, spaces):
        gathers[d - 1].wait_recv()
        value = value + dot_t(ctl_in[d - 1], dense[space_at(-d)])
    updates[...] = value
    first, sent_one = gradient(0, control[...].astype(F32))
    first_ref[...] = first
    step_src[...] = control[...].astype(F32) - descent_step * first
    again = [
        send(step_src, step_in.at[d - 1], g_s.at[1, d - 1], g_r.at[1, d - 1], {"space": space_at(d)})
        for d in range(1, spaces)
    ]

    def spread(x, table):
        up, down = halves(x)
        both = dot_t(jnp.concatenate([up, down], axis=0), table)
        return both[:rows] + both[rows:]

    updates[...] = spread(step_src[...], dense[me])
    for d in range(1, spaces):
        again[d - 1].wait_recv()
        updates[...] += spread(step_in[d - 1], dense[space_at(-d)])
    second, sent_two = gradient(1, step_src[...])
    second_ref[...] = second
    for copy in gathers + list(moved.values()) + sent_one + again + sent_two:
        copy.wait_send()


def per_device(control, block_lists, loc_tiles, ensemble, obs_col, obs_wts, innovation, inv_error):
    rows, width = control.shape
    cells = ensemble.shape[2]
    nobs = obs_col.shape[1]
    spaces, slots = lax.axis_size("space"), lax.axis_size("slot")
    chips = slots // CORES
    dma = pltpu.SemaphoreType.DMA
    vmem = pl.BlockSpec(memory_space=pltpu.VMEM)
    out = jax.ShapeDtypeStruct((rows, width), F32)
    return pl.pallas_call(
        functools.partial(kernel, spaces, slots),
        out_shape=(out, out),
        in_specs=[
            vmem, pl.BlockSpec(memory_space=pltpu.SMEM), vmem, pl.BlockSpec(memory_space=pl.ANY),
            vmem, vmem, vmem, vmem,
        ],
        out_specs=(vmem, vmem),
        scratch_shapes=[
            pltpu.VMEM((slots, rows, cells), BF16),
            pltpu.VMEM((spaces, cells, width), BF16),
            pltpu.VMEM((nobs // OBS_CHUNK, cells, OBS_CHUNK), BF16),
            pltpu.VMEM((rows, cells), F32),
            pltpu.VMEM((LEV, cells), F32),
            pltpu.VMEM((2 * rows, cells), BF16),
            pltpu.VMEM((2, chips, LEV, cells), F32),
            pltpu.VMEM((2, chips, LEV, cells), F32),
            pltpu.VMEM((2, chips, LEV, cells), F32),
            pltpu.VMEM((2, chips - 1, LEV, cells), F32),
            pltpu.VMEM((2, slots, LEV, cells), F32),
            pltpu.VMEM((2, spaces - 1, rows, width), F32),
            pltpu.VMEM((2, spaces - 1, rows, width), F32),
            pltpu.VMEM((rows, width), F32),
            pltpu.VMEM((spaces - 1, rows, width), BF16),
            pltpu.VMEM((spaces - 1, rows, width), F32),
            dma, dma((slots - 1,)), dma((slots - 1,)),
            dma((2, chips)), dma((2, chips)),
            dma((2, chips - 1)), dma((2, chips - 1)),
            dma((2, chips)), dma((2, chips)),
            dma((2, chips - 1)), dma((2, chips - 1)),
            dma((2, spaces - 1)), dma((2, spaces - 1)),
            dma((2, spaces - 1)), dma((2, spaces - 1)),
        ],
        compiler_params=pltpu.CompilerParams(
            collective_id=0, has_side_effects=True, vmem_limit_bytes=58 * 1024 * 1024
        ),
        name="envar_gradients",
    )(control, block_lists, loc_tiles, ensemble, obs_col, obs_wts, innovation, inv_error)


def solution(mesh):
    placed = (
        P("slot", "space"),
        P("space", None),
        P("space", None, None, None),
        P("slot", None, "space"),
        P("slot", "space"),
        P("slot", None, "space"),
        P("slot", "space"),
        P("slot", "space"),
    )
    return jax.shard_map(
        per_device,
        mesh=mesh,
        in_specs=placed,
        out_specs=(P("slot", "space"), P("slot", "space")),
        check_vma=False,
    )
```

time: 314 us -> 195 us (0.62)
  waiting for transfers between devices: 218 us -> 0 us
  Pallas kernels: 0 us -> 188 us
  matrix products: 26.5 us -> 0 us
  blocking collectives: 23.8 us -> 0 us
  other arithmetic: 22.1 us -> 0 us
  between operations: 14.4 us -> 0.64 us
  starting transfers between devices: 6.76 us -> 0 us
    pallas_call x0 -> x1, Pallas kernels: none -> 188 us  [per_device(): pl.pallas_call(functools.partial(kernel, spaces, slots), out_shape=(out,...]
    reduce_scatter x4 -> x0, waiting for transfers between devices: 119 us -> none  [the longest x2 67.5 us: gradient(): lax.psum_scatter(partial, 'slot', scatter_dimension=0, tiled=True)[0]]
    all_to_all x1 -> x0, waiting for transfers between devices: 52.9 us -> none  [per_device(): spread = lax.all_to_all(ensemble.reshape(slots, rows, cells), 'slot', 0, 0)]
    all_gather x2 -> x0, waiting for transfers between devices: 46 us -> none  [gradient(): everyone = lax.all_gather(adjoint, 'slot', axis=0)]
    dot_general x15 -> x0, matrix products: 26.5 us -> none  [mm(): return lax.dot_general(a, b, (dims, ((), ())), preferred_element_type=F32)]
    all_gather x2 -> x0, blocking collectives: 23.8 us -> none  [the longest x1 12.7 us: per_device(): whole = lax.all_gather(control, 'space', axis=1, tiled=True)]
    reduce_sum x5 -> x0, other arithmetic: 18.7 us -> none  [the longest x2 11.2 us: gradient(): partial = jnp.sum(spread.astype(F32) * updates, axis=1)]
    all_to_all x1 -> x0, starting transfers between devices: 6.34 us -> none  [per_device(): spread = lax.all_to_all(ensemble.reshape(slots, rows, cells), 'slot', 0, 0)]
  transfers between devices with their start and end apart: 7 -> 0, of which waited for: 7 -> 0; matrix products, arithmetic and copies ran while one was open for 2% -> 0% of each run, Pallas kernels for 0% -> 0%
where the time goes in v2:
time: 195 us; the launch traced here: 194 us
  Pallas kernels  188 us (96%)
  local copies, waits for them, and re-layouts  4.58 us (2%)
    pallas_call x1, Pallas kernels, per_device(): pl.pallas_call(functools.partial(kernel, spaces, slots), out_shape=(out,...  188 us
    unnamed x3, local copies, waits for them, and re-layouts  4.58 us

profile of v2, /device:TPU:0, one launch (start us, length us, event | category | flops | bytes accessed | tf_op | source)
XLA Modules:
  0.0 193.6 jit_solution(4670638484198478098)
XLA Ops:
  0.6 1.3 copy.10.lists
  2.0 188.4 %envar_gradients.1 = (f32[192,256]{1,0:T(8,128)}, f32[192,256]{1,0:T(8,128)}) custom-call(bf16[192,256]{1,0:T(8,128)(2,1)} %control.1, s32[8,2]{1,0:T(8,128)} %copy.10.lists, bf16[8,2,128,128]{3,2,1,0:T(8,128)(2,1)} %tiles.1, bf16[1,1536,1024]{2,1,0:T(8,128)(2,1)} %ensemble.1, s32[1,2048]{1,0:T(1,128)} %cols.1, f32[1,48,2048]{2,1,0:T(8,128)} %wts.1, ...), custom_call_target="tpu_custom_call" | custom-call | tf_op jit(solution)/shard_map/envar_gradients/pallas_call | solution.py:290
  190.4 1.6 copy.13
  192.0 1.6 copy.14

commit v3 on v2

v3 whole, which is shorter than its diff:
```python
import functools

import jax
import jax.numpy as jnp
from jax import lax
from jax.experimental import pallas as pl
from jax.experimental.pallas import tpu as pltpu
from jax.sharding import PartitionSpec as P

LEV = 48
BLOCK = 128
CORES = 2
CHUNK = 512
GROUP = 16
OBS_CHUNK = 512
descent_step = 0.5
F32 = jnp.float32
BF16 = jnp.bfloat16
MESH = pl.DeviceIdType.MESH


def halves(x):
    high = x.astype(BF16)
    return high, (x - high.astype(F32)).astype(BF16)


def dot(a, b):
    return lax.dot_general(a, b, (((1,), (0,)), ((), ())), preferred_element_type=F32)


def dot_t(a, b):
    return lax.dot_general(a, b, (((1,), (1,)), ((), ())), preferred_element_type=F32)


def staged(stages, count):
    for tick in range(count + len(stages) - 1):
        for place in reversed(range(len(stages))):
            if 0 <= tick - place < count:
                stages[place](tick - place)


def kernel(
    spaces, slots,
    control, lists, tiles, ensemble, cols, wts, innovation, inverse,
    first_ref, second_ref,
    ens, dense, pick, updates, pair, adjsum, forced, out_a, in_a, sums, in_b, adj, term, term_in,
    base, step, ctl_in, step_in,
    local_sem, ens_s, ens_r, ctl_s, ctl_r, a_s, a_r, b_s, b_r, c_s, c_r, o_s, o_r, d_s, d_r,
    g_s, g_r, t_s, t_r,
):
    rows, width = control.shape
    members, cells = ensemble.shape[1], ensemble.shape[3]
    nobs = cols.shape[1]
    chips = slots // CORES
    part = members * GROUP
    groups = LEV // GROUP
    me = lax.axis_index("space")
    slot = lax.axis_index("slot")
    z, core = slot // CORES, lax.rem(slot, CORES)
    sibling = {"slot": slot + 1 - 2 * core}

    def slot_at(dz, dk):
        zz = lax.rem(z + dz + chips, chips)
        return zz * CORES + (core if dk == 0 else 1 - core)

    def space_at(d):
        return lax.rem(me + d + spaces, spaces)

    barrier = pltpu.get_barrier_semaphore()
    for dz in range(chips):
        for dk in range(CORES):
            if dz or dk:
                pl.semaphore_signal(
                    barrier, inc=1, device_id={"slot": slot_at(dz, dk)}, device_id_type=MESH
                )
    for d in range(1, spaces):
        pl.semaphore_signal(barrier, inc=1, device_id={"space": space_at(d)}, device_id_type=MESH)
    pl.semaphore_wait(barrier, slots - 1 + spaces - 1)

    started = []

    def send(src, dst, ssem, rsem, where):
        copy = pltpu.make_async_remote_copy(
            src_ref=src, dst_ref=dst, send_sem=ssem, recv_sem=rsem,
            device_id=where, device_id_type=MESH,
        )
        copy.start()
        started.append(copy)
        return copy

    gathers = [
        send(control, ctl_in.at[d - 1], ctl_s.at[d - 1], ctl_r.at[d - 1], {"space": space_at(d)})
        for d in range(1, spaces)
    ]
    moved = {}
    for dk in (1, 0):
        for dz in sorted(range(chips), key=lambda v: -min(v, chips - v)):
            if dz or dk:
                rel = dk * chips + dz
                to = slot_at(dz, dk)
                moved[rel] = send(
                    ensemble.at[to], ens.at[rel], ens_s.at[rel - 1], ens_r.at[rel - 1], {"slot": to}
                )
    own = pltpu.make_async_copy(ensemble.at[slot], ens.at[0], local_sem)
    own.start()

    per = width // BLOCK

    def build_dense(g, carry):
        one = lists[g, 0]
        two = lists[g, 1]
        tile_one = tiles[g, 0].astype(F32)
        tile_two = tiles[g, 1].astype(F32)
        at = pl.ds(pl.multiple_of(g * BLOCK, BLOCK), BLOCK)
        for b in range(spaces * per):
            mask_one = jnp.where(one == b, 1.0, 0.0)
            mask_two = jnp.where(two == b, 1.0, 0.0)
            value = tile_one * mask_one + tile_two * mask_two
            dense[b // per, at, (b % per) * BLOCK : (b % per + 1) * BLOCK] = value.astype(BF16)
        return carry

    lax.fori_loop(0, cells // BLOCK, build_dense, 0)

    first_cell = me * cells

    def build_pick(q, carry):
        line = cols[:, pl.ds(pl.multiple_of(q * OBS_CHUNK, OBS_CHUNK), OBS_CHUNK)] - first_cell

        def band(r, inner):
            rowid = lax.broadcasted_iota(jnp.int32, (BLOCK, OBS_CHUNK), 0) + r * BLOCK
            hot = jnp.where(rowid == line, 1.0, 0.0).astype(BF16)
            pick[q, pl.ds(pl.multiple_of(r * BLOCK, BLOCK), BLOCK)] = hot
            return inner

        return lax.fori_loop(0, cells // BLOCK, band, carry)

    lax.fori_loop(0, nobs // OBS_CHUNK, build_pick, 0)

    def chunks(body):
        def run(c, carry):
            body(pl.ds(pl.multiple_of(c * CHUNK, CHUNK), CHUNK))
            return carry

        lax.fori_loop(0, cells // CHUNK, run, 0)

    def levels(g):
        return slice(g * GROUP, (g + 1) * GROUP)

    def member(m):
        return slice(m * GROUP, (m + 1) * GROUP)

    def project(g, rel, at):
        total = None
        for m in range(members):
            value = ens[rel, m, levels(g), at].astype(F32) * updates[g, member(m), at]
            total = value if total is None else total + value
        return total

    def arrive(dk):
        for dz in range(chips):
            rel = dk * chips + dz
            if rel:
                moved[rel].wait_recv()
            else:
                own.wait()

    at_a, at_b, at_c, at_o, at_d, at_g, at_t = {}, {}, {}, {}, {}, {}, {}

    def stage_a(i, g):
        if i == 0 and g == 0:
            arrive(1)

        def fill(at):
            for dz in range(chips):
                out_a[i, g, dz, :, at] = project(g, chips + dz, at)

        chunks(fill)
        at_a[i, g] = send(out_a.at[i, g], in_a.at[i, g], a_s.at[i, g], a_r.at[i, g], sibling)

    def stage_b(i, g):
        if i == 0 and g == 0:
            arrive(0)
        at_a[i, g].wait_recv()

        def fold(at):
            for dz in range(chips):
                sums[i, g, dz, :, at] = project(g, dz, at) + in_a[i, g, dz, :, at]

        chunks(fold)
        for dz in range(1, chips):
            at_b[i, g, dz] = send(
                sums.at[i, g, dz], in_b.at[i, g, dz - 1], b_s.at[i, g, dz - 1],
                b_r.at[i, g, dz - 1], {"slot": slot_at(-dz, 0)},
            )

    def stage_sum(i, g):
        for dz in range(1, chips):
            at_b[i, g, dz].wait_recv()
        total = sums[i, g, 0]
        for dz in range(1, chips):
            total = total + in_b[i, g, dz - 1]
        high, low = halves(total)
        pair[levels(g)] = high
        pair[LEV + g * GROUP : LEV + (g + 1) * GROUP] = low

    def observe_all():
        adjsum[...] = jnp.zeros_like(adjsum)

        def observe(q, carry):
            at = pl.ds(pl.multiple_of(q * OBS_CHUNK, OBS_CHUNK), OBS_CHUNK)
            table = pick[q]
            seen = dot(pair[...], table)
            seen = seen[:LEV] + seen[LEV:]
            w = wts[0, :, at]
            modelled = jnp.sum(w * seen, axis=0, keepdims=True)
            residual = inverse[:, at] * (modelled - innovation[:, at])
            up, down = halves(w * residual)
            back = dot_t(jnp.concatenate([up, down], axis=0), table)
            adjsum[...] += back[:LEV] + back[LEV:]
            return carry

        lax.fori_loop(0, nobs // OBS_CHUNK, observe, 0)

    def stage_c(i, g):
        adj[i, g, 0] = adjsum[levels(g)]
        for dz in range(1, chips):
            at_c[i, g, dz] = send(
                adj.at[i, g, 0], adj.at[i, g, dz], c_s.at[i, g, dz - 1], c_r.at[i, g, dz - 1],
                {"slot": slot_at(dz, 0)},
            )
        at_o[i, g] = send(
            adj.at[i, g, 0], adj.at[i, g, chips], o_s.at[i, g], o_r.at[i, g], sibling
        )

    def stage_d(i, g):
        for dz in range(1, chips):
            at_c[i, g, dz].wait_recv()
        at_d[i, g] = send(
            adj.at[i, g, pl.ds(1, chips - 1)], adj.at[i, g, pl.ds(chips + 1, chips - 1)],
            d_s.at[i, g], d_r.at[i, g], sibling,
        )

    def stage_force(i, g):
        at_o[i, g].wait_recv()
        at_d[i, g].wait_recv()

        def force(at):
            for m in range(members):
                total = ens[0, m, levels(g), at].astype(F32) * adj[i, g, 0, :, at]
                for rel in range(1, slots):
                    total = total + ens[rel, m, levels(g), at].astype(F32) * adj[i, g, rel, :, at]
                up, down = halves(total)
                forced[g, member(m), at] = up
                forced[g, part + m * GROUP : part + (m + 1) * GROUP, at] = down

        chunks(force)
        for d in range(1, spaces):
            to = space_at(d)
            both = dot(forced[g], dense[to])
            term[i, g, d - 1] = both[:part] + both[part:]
            at_t[i, g, d] = send(
                term.at[i, g, d - 1], term_in.at[i, g, d - 1], t_s.at[i, g, d - 1],
                t_r.at[i, g, d - 1], {"space": to},
            )
        both = dot(forced[g], dense[me])
        base[g] += both[:part] + both[part:]

    def stage_total(i, g):
        total = base[g]
        for d in range(1, spaces):
            at_t[i, g, d].wait_recv()
            total = total + term_in[i, g, d - 1]
        target = second_ref if i else first_ref
        for m in range(members):
            target[m * LEV + g * GROUP : m * LEV + (g + 1) * GROUP] = total[member(m)]
        if i == 0:
            for m in range(members):
                at = slice(m * LEV + g * GROUP, m * LEV + (g + 1) * GROUP)
                step[g, member(m)] = control[at].astype(F32) - descent_step * total[member(m)]
            for d in range(1, spaces):
                at_g[g, d] = send(
                    step.at[g], step_in.at[g, d - 1], g_s.at[g, d - 1], g_r.at[g, d - 1],
                    {"space": space_at(d)},
                )

    def spread(x, table):
        up, down = halves(x)
        both = dot_t(jnp.concatenate([up, down], axis=0), table)
        return both[:part] + both[part:]

    def stage_update(g):
        base[g] = step[g]
        updates[g] = spread(step[g], dense[me])
        for d in range(1, spaces):
            at_g[g, d].wait_recv()
            updates[g] += spread(step_in[g, d - 1], dense[space_at(-d)])

    value = dot_t(control[...], dense[me])
    for d in range(1, spaces):
        gathers[d - 1].wait_recv()
        value = value + dot_t(ctl_in[d - 1], dense[space_at(-d)])
    for g in range(groups):
        for m in range(members):
            at = slice(m * LEV + g * GROUP, m * LEV + (g + 1) * GROUP)
            updates[g, member(m)] = value[at]
            base[g, member(m)] = control[at].astype(F32)

    def on(stage, i):
        return functools.partial(stage, i)

    staged([on(stage_a, 0), on(stage_b, 0), on(stage_sum, 0)], groups)
    observe_all()
    for g in range(groups):
        stage_c(0, g)
    staged(
        [
            on(stage_d, 0), on(stage_force, 0), on(stage_total, 0), stage_update,
            on(stage_a, 1), on(stage_b, 1), on(stage_sum, 1),
        ],
        groups,
    )
    observe_all()
    for g in range(groups):
        stage_c(1, g)
    staged([on(stage_d, 1), on(stage_force, 1), on(stage_total, 1)], groups)
    for copy in started:
        copy.wait_send()


def per_device(control, block_lists, loc_tiles, ensemble, obs_col, obs_wts, innovation, inv_error):
    rows, width = control.shape
    cells = ensemble.shape[2]
    nobs = obs_col.shape[1]
    spaces, slots = lax.axis_size("space"), lax.axis_size("slot")
    chips = slots // CORES
    members = rows // LEV
    groups, part = LEV // GROUP, members * GROUP
    dma = pltpu.SemaphoreType.DMA
    vmem = pl.BlockSpec(memory_space=pltpu.VMEM)
    out = jax.ShapeDtypeStruct((rows, width), F32)
    return pl.pallas_call(
        functools.partial(kernel, spaces, slots),
        out_shape=(out, out),
        in_specs=[
            vmem, pl.BlockSpec(memory_space=pltpu.SMEM), vmem, pl.BlockSpec(memory_space=pl.ANY),
            vmem, vmem, vmem, vmem,
        ],
        out_specs=(vmem, vmem),
        scratch_shapes=[
            pltpu.VMEM((slots, members, LEV, cells), BF16),
            pltpu.VMEM((spaces, cells, width), BF16),
            pltpu.VMEM((nobs // OBS_CHUNK, cells, OBS_CHUNK), BF16),
            pltpu.VMEM((groups, part, cells), F32),
            pltpu.VMEM((2 * LEV, cells), BF16),
            pltpu.VMEM((LEV, cells), F32),
            pltpu.VMEM((groups, 2 * part, cells), BF16),
            pltpu.VMEM((2, groups, chips, GROUP, cells), F32),
            pltpu.VMEM((2, groups, chips, GROUP, cells), F32),
            pltpu.VMEM((2, groups, chips, GROUP, cells), F32),
            pltpu.VMEM((2, groups, chips - 1, GROUP, cells), F32),
            pltpu.VMEM((2, groups, slots, GROUP, cells), F32),
            pltpu.VMEM((2, groups, spaces - 1, part, width), F32),
            pltpu.VMEM((2, groups, spaces - 1, part, width), F32),
            pltpu.VMEM((groups, part, width), F32),
            pltpu.VMEM((groups, part, width), F32),
            pltpu.VMEM((spaces - 1, rows, width), BF16),
            pltpu.VMEM((groups, spaces - 1, part, width), F32),
            dma, dma((slots - 1,)), dma((slots - 1,)),
            dma((spaces - 1,)), dma((spaces - 1,)),
            dma((2, groups)), dma((2, groups)),
            dma((2, groups, chips - 1)), dma((2, groups, chips - 1)),
            dma((2, groups, chips - 1)), dma((2, groups, chips - 1)),
            dma((2, groups)), dma((2, groups)),
            dma((2, groups)), dma((2, groups)),
            dma((groups, spaces - 1)), dma((groups, spaces - 1)),
            dma((2, groups, spaces - 1)), dma((2, groups, spaces - 1)),
        ],
        compiler_params=pltpu.CompilerParams(
            collective_id=0, has_side_effects=True, vmem_limit_bytes=58 * 1024 * 1024
        ),
        name="envar_gradients",
    )(
        control, block_lists, loc_tiles, ensemble.reshape(slots, members, LEV, cells), obs_col,
        obs_wts, innovation, inv_error,
    )


def solution(mesh):
    placed = (
        P("slot", "space"),
        P("space", None),
        P("space", None, None, None),
        P("slot", None, "space"),
        P("slot", "space"),
        P("slot", None, "space"),
        P("slot", "space"),
        P("slot", "space"),
    )
    return jax.shard_map(
        per_device,
        mesh=mesh,
        in_specs=placed,
        out_specs=(P("slot", "space"), P("slot", "space")),
        check_vma=False,
    )
```

time: 195 us -> 190 us (0.974)
  Pallas kernels: 188 us -> 183 us
    pallas_call x1, Pallas kernels: 188 us -> 183 us  [per_device(): pl.pallas_call(functools.partial(kernel, spaces, slots), out_shape=(out,...]
where the time goes in v3:
time: 190 us; the launch traced here: 189 us
  Pallas kernels  183 us (96%)
  local copies, waits for them, and re-layouts  4.58 us (2%)
    pallas_call x1, Pallas kernels, per_device(): pl.pallas_call(functools.partial(kernel, spaces, slots), out_shape=(out,...  183 us
    unnamed x3, local copies, waits for them, and re-layouts  4.58 us

profile of v3, /device:TPU:0, one launch (start us, length us, event | category | flops | bytes accessed | tf_op | source)
XLA Modules:
  0.0 188.5 jit_solution(3832653994395492603)
XLA Ops:
  0.6 1.3 copy.10.lists
  2.0 183.3 %envar_gradients.1 = (f32[192,256]{1,0:T(8,128)}, f32[192,256]{1,0:T(8,128)}) custom-call(bf16[192,256]{1,0:T(8,128)(2,1)} %control.1, s32[8,2]{1,0:T(8,128)} %copy.10.lists, bf16[8,2,128,128]{3,2,1,0:T(8,128)(2,1)} %tiles.1, bf16[8,4,48,1024]{3,2,1,0:T(8,128)(2,1)} %bitcast.1, s32[1,2048]{1,0:T(1,128)} %cols.1, f32[1,48,2048]{2,1,0:T(8,128)} %wts.1, ...), custom_call_target="tpu_custom_call" | custom-call | tf_op jit(solution)/shard_map/envar_gradients/pallas_call | solution.py:341
  185.3 1.6 copy.13
  186.9 1.6 copy.14

commit v4 on v3

--- a/solution.py
+++ b/solution.py
@@ -28,10 +28,6 @@
     return lax.dot_general(a, b, (((1,), (0,)), ((), ())), preferred_element_type=F32)
 
 
-def dot_t(a, b):
-    return lax.dot_general(a, b, (((1,), (1,)), ((), ())), preferred_element_type=F32)
-
-
 def staged(stages, count):
     for tick in range(count + len(stages) - 1):
         for place in reversed(range(len(stages))):
@@ -43,7 +39,7 @@
     spaces, slots,
     control, lists, tiles, ensemble, cols, wts, innovation, inverse,
     first_ref, second_ref,
-    ens, dense, pick, updates, pair, adjsum, forced, out_a, in_a, sums, in_b, adj, term, term_in,
+    ens, dense, dense_t, pick, pick_t, updates, pair, adjsum, forced, out_a, in_a, sums, in_b, adj, term, term_in,
     base, step, ctl_in, step_in,
     local_sem, ens_s, ens_r, ctl_s, ctl_r, a_s, a_r, b_s, b_r, c_s, c_r, o_s, o_r, d_s, d_r,
     g_s, g_r, t_s, t_r,
@@ -111,12 +107,15 @@
         two = lists[g, 1]
         tile_one = tiles[g, 0].astype(F32)
         tile_two = tiles[g, 1].astype(F32)
+        flip_one, flip_two = tile_one.T, tile_two.T
         at = pl.ds(pl.multiple_of(g * BLOCK, BLOCK), BLOCK)
         for b in range(spaces * per):
             mask_one = jnp.where(one == b, 1.0, 0.0)
             mask_two = jnp.where(two == b, 1.0, 0.0)
             value = tile_one * mask_one + tile_two * mask_two
             dense[b // per, at, (b % per) * BLOCK : (b % per + 1) * BLOCK] = value.astype(BF16)
+            value = flip_one * mask_one + flip_two * mask_two
+            dense_t[b // per, (b % per) * BLOCK : (b % per + 1) * BLOCK, at] = value.astype(BF16)
         return carry
 
     lax.fori_loop(0, cells // BLOCK, build_dense, 0)
@@ -128,8 +127,10 @@
 
         def band(r, inner):
             rowid = lax.broadcasted_iota(jnp.int32, (BLOCK, OBS_CHUNK), 0) + r * BLOCK
-            hot = jnp.where(rowid == line, 1.0, 0.0).astype(BF16)
-            pick[q, pl.ds(pl.multiple_of(r * BLOCK, BLOCK), BLOCK)] = hot
+            hot = jnp.where(rowid == line, 1.0, 0.0)
+            at = pl.ds(pl.multiple_of(r * BLOCK, BLOCK), BLOCK)
+            pick[q, at] = hot.astype(BF16)
+            pick_t[q, :, at] = hot.T.astype(BF16)
             return inner
 
         return lax.fori_loop(0, cells // BLOCK, band, carry)
@@ -215,7 +216,7 @@
             modelled = jnp.sum(w * seen, axis=0, keepdims=True)
             residual = inverse[:, at] * (modelled - innovation[:, at])
             up, down = halves(w * residual)
-            back = dot_t(jnp.concatenate([up, down], axis=0), table)
+            back = dot(jnp.concatenate([up, down], axis=0), pick_t[q])
             adjsum[...] += back[:LEV] + back[LEV:]
             return carry
 
@@ -285,20 +286,20 @@
 
     def spread(x, table):
         up, down = halves(x)
-        both = dot_t(jnp.concatenate([up, down], axis=0), table)
+        both = dot(jnp.concatenate([up, down], axis=0), table)
         return both[:part] + both[part:]
 
     def stage_update(g):
         base[g] = step[g]
-        updates[g] = spread(step[g], dense[me])
+        updates[g] = spread(step[g], dense_t[me])
         for d in range(1, spaces):
             at_g[g, d].wait_recv()
-            updates[g] += spread(step_in[g, d - 1], dense[space_at(-d)])
-
-    value = dot_t(control[...], dense[me])
+            updates[g] += spread(step_in[g, d - 1], dense_t[space_at(-d)])
+
+    value = dot(control[...], dense_t[me])
     for d in range(1, spaces):
         gathers[d - 1].wait_recv()
-        value = value + dot_t(ctl_in[d - 1], dense[space_at(-d)])
+        value = value + dot(ctl_in[d - 1], dense_t[space_at(-d)])
     for g in range(groups):
         for m in range(members):
             at = slice(m * LEV + g * GROUP, m * LEV + (g + 1) * GROUP)
@@ -310,19 +311,15 @@
 
     staged([on(stage_a, 0), on(stage_b, 0), on(stage_sum, 0)], groups)
     observe_all()
-    for g in range(groups):
-        stage_c(0, g)
     staged(
         [
-            on(stage_d, 0), on(stage_force, 0), on(stage_total, 0), stage_update,
+            on(stage_c, 0), on(stage_d, 0), on(stage_force, 0), on(stage_total, 0), stage_update,
             on(stage_a, 1), on(stage_b, 1), on(stage_sum, 1),
         ],
         groups,
     )
     observe_all()
-    for g in range(groups):
-        stage_c(1, g)
-    staged([on(stage_d, 1), on(stage_force, 1), on(stage_total, 1)], groups)
+    staged([on(stage_c, 1), on(stage_d, 1), on(stage_force, 1), on(stage_total, 1)], groups)
     for copy in started:
         copy.wait_send()
 
@@ -349,7 +346,9 @@
         scratch_shapes=[
             pltpu.VMEM((slots, members, LEV, cells), BF16),
             pltpu.VMEM((spaces, cells, width), BF16),
+            pltpu.VMEM((spaces, width, cells), BF16),
             pltpu.VMEM((nobs // OBS_CHUNK, cells, OBS_CHUNK), BF16),
+            pltpu.VMEM((nobs // OBS_CHUNK, OBS_CHUNK, cells), BF16),
             pltpu.VMEM((groups, part, cells), F32),
             pltpu.VMEM((2 * LEV, cells), BF16),
             pltpu.VMEM((LEV, cells), F32),

time: 190 us -> 186 us (0.979)
  Pallas kernels: 183 us -> 181 us
    pallas_call x1, Pallas kernels: 183 us -> 181 us  [per_device(): pl.pallas_call(functools.partial(kernel, spaces, slots), out_shape=(out,...]
where the time goes in v4:
time: 186 us
  Pallas kernels  181 us (97%)
  local copies, waits for them, and re-layouts  4.58 us (2%)
    pallas_call x1, Pallas kernels, per_device(): pl.pallas_call(functools.partial(kernel, spaces, slots), out_shape=(out,...  181 us
    unnamed x3, local copies, waits for them, and re-layouts  4.58 us

profile of v4, /device:TPU:0, one launch (start us, length us, event | category | flops | bytes accessed | tf_op | source)
XLA Modules:
  0.0 186.0 jit_solution(17642275624765570665)
XLA Ops:
  0.6 1.3 copy.10.lists
  2.0 180.8 %envar_gradients.1 = (f32[192,256]{1,0:T(8,128)}, f32[192,256]{1,0:T(8,128)}) custom-call(bf16[192,256]{1,0:T(8,128)(2,1)} %control.1, s32[8,2]{1,0:T(8,128)} %copy.10.lists, bf16[8,2,128,128]{3,2,1,0:T(8,128)(2,1)} %tiles.1, bf16[8,4,48,1024]{3,2,1,0:T(8,128)(2,1)} %bitcast.1, s32[1,2048]{1,0:T(1,128)} %cols.1, f32[1,48,2048]{2,1,0:T(8,128)} %wts.1, ...), custom_call_target="tpu_custom_call" | custom-call | tf_op jit(solution)/shard_map/envar_gradients/pallas_call | solution.py:338
  182.7 1.6 copy.13
  184.4 1.6 copy.14
